TPU v7x, 32 devices: a whole 2x2x4 slice. The times are simulated.
32 devices in a mesh: det: 4 (over y, x), obs: 8 (over z, core).
Axes of the slice: x: 2, y: 2, z: 4, core: 2. Of those that a mesh axis runs over, the one named last changes fastest.
Arguments:
- tod: float32 [4, 8, 8192], P('det', 'obs'), may hold values from -200 to 200
- angle: float32 [4, 8, 8192], P('det', 'obs'), may hold values from -3.140625 to 3.140625
- pix_in: int32 [4, 8, 8192], P('det', 'obs'), may hold values from 0 to 63
- tile_block: int32 [4, 8, 32], P('det', 'obs'), may hold values from 0 to 511
- base_len: int32 [4, 8, 40], P('det', 'obs'), may hold values from 1 to 384, 8192 in all within a row
- touched: int32 [8, 16], P('obs'), may hold values from 0 to 511, as said below
Outputs:
- baselines: float32 [4, 8, 40], P('det', 'obs')
- residual_rate: float32 [4, 8, 40], P('det', 'obs')
Inputs may be any that keep to these rules, and one draw needn't show every extreme that they name: `touched`: each row lists 16 distinct patches; patch p is held by owner p // 64; at most 4 patches of one row share an owner, and one owner holds exactly 4 patches of every row.
All inputs are finite; a program needn't handle non-finite values.
Results may differ from a plain program's by a relative error of at most 0.0003.
Values sent between devices are 32-bit elements; how exact they have to be, the bound alone decides.
A program may use at most 128 MiB of HBM per device.

v0:
```python
import math
import jax
import jax.numpy as jnp
from jax import lax
from jax.sharding import PartitionSpec as P

TILE = 256
BLK = 64
PATCH_PIX = 2048
PT = 16
PATCH_OWN = 64
ITERS = 2
UPPER_LIMIT = lax.Precision.HIGHEST


def pixel_inverse(hits):
    a11 = hits[:, 0] + 1.0
    a12 = hits[:, 1]
    a13 = hits[:, 2]
    a22 = hits[:, 3] + 1.0
    a23 = hits[:, 4]
    a33 = hits[:, 5] + 1.0
    c11 = a22 * a33 - a23 * a23
    c12 = a13 * a23 - a12 * a33
    c13 = a12 * a23 - a13 * a22
    c22 = a11 * a33 - a13 * a13
    c23 = a12 * a13 - a11 * a23
    c33 = a11 * a22 - a12 * a12
    determinant = a11 * c11 + a12 * c12 + a13 * c13
    return jnp.stack([c11, c12, c13, c22, c23, c33], axis=1) / determinant[:, None]


def apply_inverse(inverse, pixel_binned_map):
    first = (
        inverse[:, 0] * pixel_binned_map[:, 0]
        + inverse[:, 1] * pixel_binned_map[:, 1]
        + inverse[:, 2] * pixel_binned_map[:, 2]
    )
    second = (
        inverse[:, 1] * pixel_binned_map[:, 0]
        + inverse[:, 3] * pixel_binned_map[:, 1]
        + inverse[:, 4] * pixel_binned_map[:, 2]
    )
    third = (
        inverse[:, 2] * pixel_binned_map[:, 0]
        + inverse[:, 4] * pixel_binned_map[:, 1]
        + inverse[:, 5] * pixel_binned_map[:, 2]
    )
    return jnp.stack([first, second, third], axis=1)


def combine_det(partial_value):
    total = lax.psum(partial_value, "det")
    return total


def squares(residual_vector):
    return lax.psum(jnp.sum(residual_vector * residual_vector), ("det", "obs"))


def body(tod, angle, pix_in, tile_block, base_len, touched):
    signal = tod[0, 0]
    inner = pix_in[0, 0]
    tile_rows = tile_block[0, 0]
    lengths = base_len[0, 0]
    patch_list = touched[0]
    samples = signal.shape[0]
    nbase = lengths.shape[0]
    ntile = samples // TILE
    group = math.gcd(ntile, 64)
    groups = ntile // group
    blocks = PATCH_PIX // BLK
    local_blocks = PT * blocks
    obs_count = lax.axis_size("obs")
    cap = max(2, 2 * PT // obs_count)
    slots = obs_count * cap
    cos_w = jnp.cos(2.0 * angle[0, 0])
    sin_w = jnp.sin(2.0 * angle[0, 0])
    ends = jnp.cumsum(lengths)
    base_index = jnp.searchsorted(ends, jnp.arange(samples, dtype=jnp.int32), side="right")
    inner_groups = inner.reshape(groups, group, TILE)
    cos_groups = cos_w.reshape(groups, group, TILE)
    sin_groups = sin_w.reshape(groups, group, TILE)
    pixel_iota = jnp.arange(BLK, dtype=jnp.int32)
    tile_select = (tile_rows[None, :] == jnp.arange(local_blocks, dtype=jnp.int32)[:, None]).astype(
        jnp.float32
    )

    def tile_indicator_matrix(index):
        return (index[:, None, :] == pixel_iota[None, :, None]).astype(jnp.float32)

    def bin_local(value_entries):
        comps = value_entries.shape[0]
        grouped = value_entries.reshape(comps, groups, group, TILE).transpose(1, 2, 0, 3)

        def bin_one_group(index_couple):
            return jnp.einsum(
                "awv,agv->awg",
                index_couple[0],
                tile_indicator_matrix(index_couple[1]),
                precision=UPPER_LIMIT,
            )

        per_tile = lax.map(bin_one_group, (grouped, inner_groups)).reshape(ntile, comps * BLK)
        summed = jnp.dot(tile_select, per_tile, precision=UPPER_LIMIT)
        return (
            summed.reshape(PT, blocks, comps, BLK)
            .transpose(0, 2, 1, 3)
            .reshape(PT, comps, PATCH_PIX)
        )

    def unbin_local(local_map):
        rows = (
            local_map.reshape(PT, 3, blocks, BLK)
            .transpose(0, 2, 1, 3)
            .reshape(local_blocks, 3 * BLK)
        )
        picked = jnp.take(rows, tile_rows, axis=0).reshape(groups, group, 3, BLK)

        def unbin_one_group(partition_pieces):
            value_entries = jnp.einsum(
                "jwx,jxd->jwd",
                partition_pieces[0],
                tile_indicator_matrix(partition_pieces[1]),
                precision=UPPER_LIMIT,
            )
            return (
                value_entries[:, 0]
                + partition_pieces[2] * value_entries[:, 1]
                + partition_pieces[3] * value_entries[:, 2]
            )

        return lax.map(unbin_one_group, (picked, inner_groups, cos_groups, sin_groups)).reshape(
            samples
        )

    owner_of = patch_list // PATCH_OWN
    slot_of = patch_list % PATCH_OWN
    positions = jnp.arange(PT, dtype=jnp.int32)
    before = (owner_of[None, :] == owner_of[:, None]) & (positions[None, :] < positions[:, None])
    rank = jnp.sum(before.astype(jnp.int32), axis=1)
    target = owner_of * cap + rank
    placed = target[None, :] == jnp.arange(slots, dtype=jnp.int32)[:, None]
    packing = placed.astype(jnp.float32)
    send_ids = (jnp.sum(jnp.where(placed, slot_of[None, :] + 1, 0), axis=1) - 1).reshape(
        obs_count, cap
    )

    def pack_map(total):
        comps, width = (total.shape[1], total.shape[2])
        return jnp.dot(packing, total.reshape(PT, comps * width), precision=UPPER_LIMIT).reshape(
            obs_count, cap, comps, width
        )

    def unpack_map(returned):
        width = returned.shape[3]
        return jnp.dot(
            packing.T, returned.reshape(slots, 3 * width), precision=UPPER_LIMIT
        ).reshape(PT, 3, width)

    ones = jnp.ones_like(signal)
    first_values = jnp.stack(
        [
            signal,
            signal * cos_w,
            signal * sin_w,
            ones,
            cos_w,
            sin_w,
            cos_w * cos_w,
            cos_w * sin_w,
            sin_w * sin_w,
        ]
    )
    first_total = combine_det(bin_local(first_values))
    received, source_ids = (
        lax.all_to_all(pack_map(first_total), "obs", split_axis=0, concat_axis=0, tiled=True),
        lax.all_to_all(send_ids, "obs", split_axis=0, concat_axis=0, tiled=True),
    )
    owner_pick = (
        source_ids.reshape(slots)[None, :] == jnp.arange(PATCH_OWN, dtype=jnp.int32)[:, None]
    ).astype(jnp.float32)

    def gather_owner(arrived):
        comps, width = (arrived.shape[2], arrived.shape[3])
        return jnp.dot(
            owner_pick, arrived.reshape(slots, comps * width), precision=UPPER_LIMIT
        ).reshape(PATCH_OWN, comps, width)

    def return_map(owned):
        width = owned.shape[2]
        outgoing = jnp.dot(
            owner_pick.T, owned.reshape(PATCH_OWN, 3 * width), precision=UPPER_LIMIT
        ).reshape(obs_count, cap, 3, width)
        return lax.all_to_all(outgoing, "obs", split_axis=0, concat_axis=0, tiled=True)

    accumulated = gather_owner(received)
    inverse = pixel_inverse(accumulated[:, 3:])
    start_map = apply_inverse(inverse, accumulated[:, :3])
    start_local = unpack_map(return_map(start_map))
    cleaned = signal - unbin_local(start_local)
    right_side = jax.ops.segment_sum(
        cleaned, base_index, num_segments=nbase, indices_are_sorted=True
    )
    solution = jnp.zeros_like(right_side)
    residual_vector = right_side
    direction = right_side
    norm_now = squares(residual_vector)
    for step in range(ITERS):
        expanded = jnp.take(direction, base_index)
        apply_value_entries = jnp.stack([expanded, expanded * cos_w, expanded * sin_w])
        apply_total = combine_det(bin_local(apply_value_entries))
        apply_arrived = lax.all_to_all(
            pack_map(apply_total), "obs", split_axis=0, concat_axis=0, tiled=True
        )
        solved = apply_inverse(inverse, gather_owner(apply_arrived))
        apply_local_map = unpack_map(return_map(solved))
        image = jax.ops.segment_sum(
            expanded - unbin_local(apply_local_map),
            base_index,
            num_segments=nbase,
            indices_are_sorted=True,
        )
        alpha = norm_now / lax.psum(jnp.sum(direction * image), ("det", "obs"))
        solution = solution + alpha * direction
        residual_vector = residual_vector - alpha * image
        if step + 1 < ITERS:
            norm_next = squares(residual_vector)
            direction = residual_vector + norm_next / norm_now * direction
            norm_now = norm_next
    rate = residual_vector / lengths.astype(jnp.float32)
    return (solution[None, None], rate[None, None])


def solution(mesh):
    placed = (
        P("det", "obs", None),
        P("det", "obs", None),
        P("det", "obs", None),
        P("det", "obs", None),
        P("det", "obs", None),
        P("obs", None),
    )
    return jax.shard_map(
        body,
        mesh=mesh,
        in_specs=placed,
        out_specs=(P("det", "obs", None), P("det", "obs", None)),
        check_vma=False,
    )
```

profile of v0, /device:TPU:12, one launch (start us, length us, event | category | flops | bytes accessed | tf_op | source)
XLA Modules:
  0.0 1070.5 jit_solution(13468639081524979222)
XLA Ops:
  23.7 49.2 %all-reduce.5.cloned.1.call-done = f32[9,2048,16]{1,2,0:T(8,128)} async-done(((f32[9,2048,16]{1,2,0:T(8,128)}), f32[9,2048,16]{1,2,0:T(8,128)}) %all-reduce.5.cloned.1.call-update) | async-done | bytes 1179664 | tf_op jit(solution)/shard_map/psum | solution.py:53
  84.3 50.0 %all-to-all-done.1 = f32[8,4,9,2048]{3,1,2,0:T(4,128)S(1)} async-done(((f32[8,4,9,2048]{3,1,2,0:T(4,128)}), f32[8,4,9,2048]{3,1,2,0:T(4,128)S(1)}, u32[]{:S(2)}, u32[]{:S(2)}) %all-to-all-start.1) | async-done | bytes 2359328 | tf_op jit(solution)/shard_map/all_to_all | solution.py:177
  150.6 312.5 %while.24 = (s32[]{:T(128)}, u32[8192]{0:T(1024)S(1)}, u32[8192]{0:T(1024)S(1)}, s32[40]{0:T(128)S(1)}, s32[]{:T(128)}, /*index=5*/s32[]{:T(128)}) while((s32[]{:T(128)}, u32[8192]{0:T(1024)S(1)}, u32[8192]{0:T(1024)S(1)}, s32[40]{0:T(128)S(1)}, s32[]{:T(128)}, /*index=5*/s32[]{:T(128)}) %tuple.233), condition=%wide.region_2.3_spmd.clone, body=%wide.region_1.2_spmd.clone.sunk | while | flops 1392643 | bytes 262864 | solution.py:80
  152.8 25.0 %fusion.141 = u32[8192]{0:T(1024)S(1)} fusion(u32[8192]{0:T(1024)S(1)} %get-tuple-element.525, u32[8192]{0:T(1024)S(1)} %get-tuple-element.524, s32[]{:T(128)} %bitcast.438, s32[]{:T(128)} %bitcast.439, s32[]{:T(128)} %bitcast.440, s32[]{:T(128)} %bitcast.441, s32[]{:T(128)} %bitcast.442, s32[]{:T(128)} %bitcast.443, s32[]{:T(128)} %bitcast.444, ...), kind=kLoop, calls=%fused_computation.8.clone.1 | loop fusion | flops 696320 | bytes 98465 | tf_op jit(solution)/shard_map/jit(searchsorted)/jit(_searchsorted_scan_impl)/vmap(jit(_searchsorted_scan_impl))/while/body/eval_jaxpr/select_n | solution.py:80
  177.7 25.0 %fusion.140 = u32[8192]{0:T(1024)S(1)} fusion(u32[8192]{0:T(1024)S(1)} %get-tuple-element.525, u32[8192]{0:T(1024)S(1)} %get-tuple-element.524, s32[]{:T(128)} %bitcast.438, s32[]{:T(128)} %bitcast.439, s32[]{:T(128)} %bitcast.440, s32[]{:T(128)} %bitcast.441, s32[]{:T(128)} %bitcast.442, s32[]{:T(128)} %bitcast.443, s32[]{:T(128)} %bitcast.444, ...), kind=kLoop, calls=%fused_computation.9.clone.1 | loop fusion | flops 696320 | bytes 98465 | tf_op jit(solution)/shard_map/jit(searchsorted)/jit(_searchsorted_scan_impl)/vmap(jit(_searchsorted_scan_impl))/while/body/eval_jaxpr/select_n | solution.py:80
  204.9 25.0 %fusion.141 = u32[8192]{0:T(1024)S(1)} fusion(u32[8192]{0:T(1024)S(1)} %get-tuple-element.525, u32[8192]{0:T(1024)S(1)} %get-tuple-element.524, s32[]{:T(128)} %bitcast.438, s32[]{:T(128)} %bitcast.439, s32[]{:T(128)} %bitcast.440, s32[]{:T(128)} %bitcast.441, s32[]{:T(128)} %bitcast.442, s32[]{:T(128)} %bitcast.443, s32[]{:T(128)} %bitcast.444, ...), kind=kLoop, calls=%fused_computation.8.clone.1 | loop fusion | flops 696320 | bytes 98465 | tf_op jit(solution)/shard_map/jit(searchsorted)/jit(_searchsorted_scan_impl)/vmap(jit(_searchsorted_scan_impl))/while/body/eval_jaxpr/select_n | solution.py:80
  229.8 25.0 %fusion.140 = u32[8192]{0:T(1024)S(1)} fusion(u32[8192]{0:T(1024)S(1)} %get-tuple-element.525, u32[8192]{0:T(1024)S(1)} %get-tuple-element.524, s32[]{:T(128)} %bitcast.438, s32[]{:T(128)} %bitcast.439, s32[]{:T(128)} %bitcast.440, s32[]{:T(128)} %bitcast.441, s32[]{:T(128)} %bitcast.442, s32[]{:T(128)} %bitcast.443, s32[]{:T(128)} %bitcast.444, ...), kind=kLoop, calls=%fused_computation.9.clone.1 | loop fusion | flops 696320 | bytes 98465 | tf_op jit(solution)/shard_map/jit(searchsorted)/jit(_searchsorted_scan_impl)/vmap(jit(_searchsorted_scan_impl))/while/body/eval_jaxpr/select_n | solution.py:80
  281.9 25.0 %fusion.140 = u32[8192]{0:T(1024)S(1)} fusion(u32[8192]{0:T(1024)S(1)} %get-tuple-element.525, u32[8192]{0:T(1024)S(1)} %get-tuple-element.524, s32[]{:T(128)} %bitcast.438, s32[]{:T(128)} %bitcast.439, s32[]{:T(128)} %bitcast.440, s32[]{:T(128)} %bitcast.441, s32[]{:T(128)} %bitcast.442, s32[]{:T(128)} %bitcast.443, s32[]{:T(128)} %bitcast.444, ...), kind=kLoop, calls=%fused_computation.9.clone.1 | loop fusion | flops 696320 | bytes 98465 | tf_op jit(solution)/shard_map/jit(searchsorted)/jit(_searchsorted_scan_impl)/vmap(jit(_searchsorted_scan_impl))/while/body/eval_jaxpr/select_n | solution.py:80
  309.0 25.0 %fusion.141 = u32[8192]{0:T(1024)S(1)} fusion(u32[8192]{0:T(1024)S(1)} %get-tuple-element.525, u32[8192]{0:T(1024)S(1)} %get-tuple-element.524, s32[]{:T(128)} %bitcast.438, s32[]{:T(128)} %bitcast.439, s32[]{:T(128)} %bitcast.440, s32[]{:T(128)} %bitcast.441, s32[]{:T(128)} %bitcast.442, s32[]{:T(128)} %bitcast.443, s32[]{:T(128)} %bitcast.444, ...), kind=kLoop, calls=%fused_computation.8.clone.1 | loop fusion | flops 696320 | bytes 98465 | tf_op jit(solution)/shard_map/jit(searchsorted)/jit(_searchsorted_scan_impl)/vmap(jit(_searchsorted_scan_impl))/while/body/eval_jaxpr/select_n | solution.py:80
  334.0 25.0 %fusion.140 = u32[8192]{0:T(1024)S(1)} fusion(u32[8192]{0:T(1024)S(1)} %get-tuple-element.525, u32[8192]{0:T(1024)S(1)} %get-tuple-element.524, s32[]{:T(128)} %bitcast.438, s32[]{:T(128)} %bitcast.439, s32[]{:T(128)} %bitcast.440, s32[]{:T(128)} %bitcast.441, s32[]{:T(128)} %bitcast.442, s32[]{:T(128)} %bitcast.443, s32[]{:T(128)} %bitcast.444, ...), kind=kLoop, calls=%fused_computation.9.clone.1 | loop fusion | flops 696320 | bytes 98465 | tf_op jit(solution)/shard_map/jit(searchsorted)/jit(_searchsorted_scan_impl)/vmap(jit(_searchsorted_scan_impl))/while/body/eval_jaxpr/select_n | solution.py:80
  361.1 25.0 %fusion.141 = u32[8192]{0:T(1024)S(1)} fusion(u32[8192]{0:T(1024)S(1)} %get-tuple-element.525, u32[8192]{0:T(1024)S(1)} %get-tuple-element.524, s32[]{:T(128)} %bitcast.438, s32[]{:T(128)} %bitcast.439, s32[]{:T(128)} %bitcast.440, s32[]{:T(128)} %bitcast.441, s32[]{:T(128)} %bitcast.442, s32[]{:T(128)} %bitcast.443, s32[]{:T(128)} %bitcast.444, ...), kind=kLoop, calls=%fused_computation.8.clone.1 | loop fusion | flops 696320 | bytes 98465 | tf_op jit(solution)/shard_map/jit(searchsorted)/jit(_searchsorted_scan_impl)/vmap(jit(_searchsorted_scan_impl))/while/body/eval_jaxpr/select_n | solution.py:80
  386.1 25.0 %fusion.140 = u32[8192]{0:T(1024)S(1)} fusion(u32[8192]{0:T(1024)S(1)} %get-tuple-element.525, u32[8192]{0:T(1024)S(1)} %get-tuple-element.524, s32[]{:T(128)} %bitcast.438, s32[]{:T(128)} %bitcast.439, s32[]{:T(128)} %bitcast.440, s32[]{:T(128)} %bitcast.441, s32[]{:T(128)} %bitcast.442, s32[]{:T(128)} %bitcast.443, s32[]{:T(128)} %bitcast.444, ...), kind=kLoop, calls=%fused_computation.9.clone.1 | loop fusion | flops 696320 | bytes 98465 | tf_op jit(solution)/shard_map/jit(searchsorted)/jit(_searchsorted_scan_impl)/vmap(jit(_searchsorted_scan_impl))/while/body/eval_jaxpr/select_n | solution.py:80
  413.2 25.0 %fusion.141 = u32[8192]{0:T(1024)S(1)} fusion(u32[8192]{0:T(1024)S(1)} %get-tuple-element.525, u32[8192]{0:T(1024)S(1)} %get-tuple-element.524, s32[]{:T(128)} %bitcast.438, s32[]{:T(128)} %bitcast.439, s32[]{:T(128)} %bitcast.440, s32[]{:T(128)} %bitcast.441, s32[]{:T(128)} %bitcast.442, s32[]{:T(128)} %bitcast.443, s32[]{:T(128)} %bitcast.444, ...), kind=kLoop, calls=%fused_computation.8.clone.1 | loop fusion | flops 696320 | bytes 98465 | tf_op jit(solution)/shard_map/jit(searchsorted)/jit(_searchsorted_scan_impl)/vmap(jit(_searchsorted_scan_impl))/while/body/eval_jaxpr/select_n | solution.py:80
  438.2 25.0 %fusion.140 = u32[8192]{0:T(1024)S(1)} fusion(u32[8192]{0:T(1024)S(1)} %get-tuple-element.525, u32[8192]{0:T(1024)S(1)} %get-tuple-element.524, s32[]{:T(128)} %bitcast.438, s32[]{:T(128)} %bitcast.439, s32[]{:T(128)} %bitcast.440, s32[]{:T(128)} %bitcast.441, s32[]{:T(128)} %bitcast.442, s32[]{:T(128)} %bitcast.443, s32[]{:T(128)} %bitcast.444, ...), kind=kLoop, calls=%fused_computation.9.clone.1 | loop fusion | flops 696320 | bytes 98465 | tf_op jit(solution)/shard_map/jit(searchsorted)/jit(_searchsorted_scan_impl)/vmap(jit(_searchsorted_scan_impl))/while/body/eval_jaxpr/select_n | solution.py:80
  479.4 57.2 %scatter_custom_fusion = f32[40]{0:T(128)S(1)} fusion(s32[8192]{0:T(1024)} %convert_element_type.34, f32[8192]{0:T(1024)S(1)} %add_subtract_fusion.2, f32[]{:T(128)} %constant.148.clone.1), kind=kCustom, calls=%fused_computation.230 | custom fusion | flops 8192 | bytes 672 | tf_op jit(solution)/shard_map/scatter-add | solution.py:202
  538.6 25.7 %fusion.114 = (f32[8192]{0:T(1024)S(1)}, f32[8192]{0:T(1024)S(1)}, pred[8192]{0:T(1024)(128)(4,1)S(1)}, pred[8192]{0:T(1024)(128)(4,1)S(1)}, pred[8192]{0:T(1024...) fusion(f32[8192]{0:T(1024)S(1)} %bitcast.499, ...), kind=kLoop, calls=%fused_computation.235 | loop fusion | flops 712704 | bytes 458912 | tf_op jit(solution)/shard_map/mul | solution.py:211
  571.7 44.1 %all-reduce.7.cloned.1.call-done = f32[3,2048,16]{1,2,0:T(8,128)} async-done(((f32[3,2048,16]{1,2,0:T(8,128)}), f32[3,2048,16]{1,2,0:T(8,128)}) %all-reduce.7.cloned.1.call-update) | async-done | bytes 393232 | tf_op jit(solution)/shard_map/psum | solution.py:53
  682.4 57.2 %scatter_custom_fusion.1 = f32[40]{0:T(128)S(1)} fusion(s32[8192]{0:T(1024)} %convert_element_type.34, f32[8192]{0:T(1024)S(1)} %add_subtract_fusion.1, f32[]{:T(128)} %constant.148.clone.1), kind=kCustom, calls=%fused_computation.228 | custom fusion | flops 8192 | bytes 672 | tf_op jit(solution)/shard_map/scatter-add | solution.py:218
  740.1 41.3 %all-reduce = (f32[]{:T(128)}, f32[]{:T(128)}) all-reduce(f32[]{:T(128)} %get-tuple-element.196, f32[]{:T(128)} %get-tuple-element.195), channel_id=1, replica_groups=mesh['det'=4,'obs'=8] {'det','obs'}, use_global_device_ids=true, to_apply=%region_8.10 | all-reduce | flops 2 | bytes 16 | tf_op jit(solution)/shard_map/psum | solution.py:58
  783.4 39.9 %psum.53 = f32[]{:T(128)} all-reduce(f32[]{:T(128)} %get-tuple-element.209), channel_id=1, replica_groups=mesh['det'=4,'obs'=8] {'det','obs'}, use_global_device_ids=true, to_apply=%region_14.17 | all-reduce | flops 1 | bytes 8 | tf_op jit(solution)/shard_map/psum | solution.py:58
  826.7 25.8 %fusion.113 = (f32[8192]{0:T(1024)S(1)}, f32[8192]{0:T(1024)S(1)}) fusion(f32[8192]{0:T(1024)S(1)} %bitcast.501, pred[8192]{0:T(1024)(128)(4,1)} %get-tuple-element.252, pred[8192]{0:T(1024)(128)(4,1)} %get-tuple-element.251, pred[8192]{0:T(1024)(128)(4,1)} %get-tuple-element.250, pred[8192]{0:T(1024)(128)(4,1)} %get-tuple-element.249, ...), kind=kLoop, calls=%fused_computation.234 | loop fusion | flops 335872 | bytes 426144 | tf_op jit(solution)/shard_map/mul | solution.py:211
  859.8 44.0 %all-reduce.9.cloned.1.call-done = f32[3,2048,16]{1,2,0:T(8,128)} async-done(((f32[3,2048,16]{1,2,0:T(8,128)}), f32[3,2048,16]{1,2,0:T(8,128)}) %all-reduce.9.cloned.1.call-update) | async-done | bytes 393232 | tf_op jit(solution)/shard_map/psum | solution.py:53
  962.1 57.2 %scatter_custom_fusion.2 = f32[40]{0:T(128)S(1)} fusion(s32[8192]{0:T(1024)} %convert_element_type.34, f32[8192]{0:T(1024)S(1)} %add_subtract_fusion, f32[]{:T(128)} %constant.148.clone.1), kind=kCustom, calls=%fused_computation.226 | custom fusion | flops 8192 | bytes 672 | tf_op jit(solution)/shard_map/scatter-add | solution.py:218
  1019.9 41.3 %psum.55 = f32[]{:T(128)} all-reduce(f32[]{:T(128)} %multiply_reduce_fusion), channel_id=1, replica_groups=mesh['det'=4,'obs'=8] {'det','obs'}, use_global_device_ids=true, to_apply=%region_18.21 | all-reduce | flops 1 | bytes 8 | tf_op jit(solution)/shard_map/psum | solution.py:224
  (196 shorter events, 244.0 us)
Async XLA Ops:
  7.2 7.1 copy-start.14
  7.2 65.7 %all-reduce.5.cloned.1.call-start = ((), (), s32[]{:S(2)}) async-start(), calls=%async_computation.7 | async-start | bytes 2359296 | tf_op jit(solution)/shard_map/psum | solution.py:53
  8.9 5.3 copy-start
  8.9 5.3 copy-start.2
  11.0 3.3 copy-start.5
  16.2 1.1 copy-start.17
  17.5 452.3 %copy-start.7 = (s32[16]{0:T(128)}, s32[16]{0:T(128)S(1)}, u32[]{:S(2)}) copy-start(s32[16]{0:T(128)S(1)} %fusion.103) | copy-start | bytes 196
  18.3 59.0 %all-to-all-start = ((s32[8,1,4]{2,1,0:T(1,128)}), s32[8,1,4]{2,1,0:T(1,128)S(1)}, u32[]{:S(2)}, u32[]{:S(2)}) async-start(s32[8,1,4]{2,1,0:T(1,128)} %bitcast.10), calls=%async_computation | async-start | bytes 8192 | tf_op jit(solution)/shard_map/all_to_all | solution.py:178
  77.3 5.9 copy-start.15
  77.3 57.0 %all-to-all-start.1 = ((f32[8,4,9,2048]{3,1,2,0:T(4,128)}), f32[8,4,9,2048]{3,1,2,0:T(4,128)S(1)}, u32[]{:S(2)}, u32[]{:S(2)}) async-start(f32[8,4,9,2048]{3,1,2,0:T(4,128)} %fusion.34), calls=%async_computation.1 | async-start | bytes 4718592 | tf_op jit(solution)/shard_map/all_to_all | solution.py:177
  142.9 320.9 %all-to-all-start.2 = ((f32[8,4,3,2048]{3,1,2,0:T(4,128)}), f32[8,4,3,2048]{3,1,2,0:T(4,128)}, u32[]{:S(2)}, u32[]{:S(2)}) async-start(f32[8,4,3,2048]{3,1,2,0:T(4,128)} %fusion.17), calls=%async_computation.2 | async-start | bytes 1572864 | tf_op jit(solution)/shard_map/all_to_all | solution.py:195
  150.5 465.4 %all-reduce.7.cloned.1.call-start = ((), (), s32[]{:S(2)}) async-start(), calls=%async_computation.8 | async-start | bytes 786432 | tf_op jit(solution)/shard_map/psum | solution.py:53
  463.8 12.8 %copy-start.10 = (s32[1024]{0:T(1024)}, s32[1024]{0:T(1024)S(1)}, u32[]{:S(2)}) copy-start(s32[1024]{0:T(1024)S(1)} %pad_clamp_fusion) | copy-start | bytes 12292
  463.8 14.5 %copy-start.11 = (pred[32]{0:T(512)(128)(4,1)}, pred[32]{0:T(512)(128)(4,1)S(1)}, u32[]{:S(2)}) copy-start(pred[32]{0:T(512)(128)(4,1)S(1)} %compare_and_fusion.1) | copy-start | bytes 100
  472.7 5.8 copy-start.6
  472.7 6.6 copy-start.1
  472.7 6.6 copy-start.3
  472.7 6.6 copy-start.4
  571.6 332.2 %all-reduce.9.cloned.1.call-start = ((), (), s32[]{:S(2)}) async-start(), calls=%async_computation.9 | async-start | bytes 786432 | tf_op jit(solution)/shard_map/psum | solution.py:53
  668.4 4.3 copy-start.8
  675.6 5.7 copy-start.12
  956.5 1.1 copy-start.9
  959.2 1.9 copy-start.13
  959.2 103.3 %copy-start.16 = (s32[1,1,40]{2,1,0:T(1,128)S(1)}, s32[1,1,40]{2,1,0:T(1,128)}, u32[]{:S(2)}) copy-start(s32[1,1,40]{2,1,0:T(1,128)} %param.16) | copy-start | bytes 484
Sparse Core Ops, SparseCore 0:
  17.4 55.4 all-reduce.4
  571.8 44.0 all-reduce.6
  860.0 43.8 all-reduce.8
where the time goes:
time: 1080 us; the launch traced here: 1070 us
  other arithmetic  534 us (49%)
  blocking collectives  217 us (20%)
  waiting for transfers between devices  187 us (17%)
  local copies, waits for them, and re-layouts  58.7 us (5%)
  matrix products  35.6 us (3%)
  between operations  19 us (2%)
  starting transfers between devices  18.9 us (2%)
    select_n x12, other arithmetic, body(): jnp.searchsorted(ends, jnp.arange(samples, dtype=jnp.int32), side='right')  300 us
    psum x3, waiting for transfers between devices, combine_det(): total = lax.psum(partial_value, 'det')  137 us
    scatter-add x2, other arithmetic, body(): jax.ops.segment_sum(expanded - unbin_local(apply_local_map), base_index,...  114 us
    psum x2, blocking collectives, squares(): return lax.psum(jnp.sum(residual_vector * residual_vector), ('det', 'obs'))  81.2 us
    scatter-add x1, other arithmetic, body(): jax.ops.segment_sum(cleaned, base_index, num_segments=nbase, indices_are_...  57.2 us
    mul x2, other arithmetic, body(): expanded * cos_w  51.5 us
    all_to_all x1, waiting for transfers between devices, body(): lax.all_to_all(pack_map(first_total), 'obs', split_axis=0, concat_axis=0,...  50 us
    all_to_all x2, blocking collectives, body(): lax.all_to_all(pack_map(apply_total), 'obs', split_axis=0, concat_axis=0,...  47.4 us
  transfers between devices with their start and end apart: 6, of which 4 were waited for; matrix products, arithmetic and copies ran while one was open for 30% of the time, Pallas kernels for 0%

commit v1 on v0

--- a/solution.py
+++ b/solution.py
@@ -3,6 +3,7 @@
 import jax.numpy as jnp
 from jax import lax
 from jax.sharding import PartitionSpec as P
+from jax.lax import all_gather
 
 TILE = 256
 BLK = 64
@@ -50,7 +51,7 @@
 
 
 def combine_det(partial_value):
-    total = lax.psum(partial_value, "det")
+    total = all_gather(partial_value, "det").sum(axis=0)
     return total
 
 

time: 1080 us -> 1070 us (level)
  waiting for transfers between devices: 187 us -> 164 us
    psum x3 -> x0, waiting for transfers between devices: 137 us -> none  [combine_det(): total = lax.psum(partial_value, 'det')]
    all_gather x0 -> x3, waiting for transfers between devices: none -> 114 us  [combine_det(): total = all_gather(partial_value, 'det').sum(axis=0)]
    another operation x1 -> x7, local copies, waits for them, and re-layouts: 0.09 us -> 14 us  [the longest x6 13.9 us: combine_det(): total = all_gather(partial_value, 'det').sum(axis=0)]
where the time goes in v1:
time: 1070 us; the launch traced here: 1060 us
  other arithmetic  541 us (51%)
  blocking collectives  217 us (20%)
  waiting for transfers between devices  164 us (15%)
  local copies, waits for them, and re-layouts  62.9 us (6%)
  matrix products  34.3 us (3%)
  starting transfers between devices  18.6 us (2%)
  between operations  18.6 us (2%)
    select_n x12, other arithmetic, body(): jnp.searchsorted(ends, jnp.arange(samples, dtype=jnp.int32), side='right')  300 us
    scatter-add x2, other arithmetic, body(): jax.ops.segment_sum(expanded - unbin_local(apply_local_map), base_index,...  114 us
    all_gather x3, waiting for transfers between devices, combine_det(): total = all_gather(partial_value, 'det').sum(axis=0)  114 us
    psum x2, blocking collectives, squares(): return lax.psum(jnp.sum(residual_vector * residual_vector), ('det', 'obs'))  81.1 us
    scatter-add x1, other arithmetic, body(): jax.ops.segment_sum(cleaned, base_index, num_segments=nbase, indices_are_...  57 us
    mul x2, other arithmetic, body(): expanded * cos_w  52.2 us
    all_to_all x1, waiting for transfers between devices, body(): lax.all_to_all(pack_map(first_total), 'obs', split_axis=0, concat_axis=0,...  50 us
    all_to_all x2, blocking collectives, body(): lax.all_to_all(pack_map(apply_total), 'obs', split_axis=0, concat_axis=0,...  47.6 us
  transfers between devices with their start and end apart: 6, of which 4 were waited for; matrix products, arithmetic and copies ran while one was open for 30% of the time, Pallas kernels for 0%

profile of v1, /device:TPU:12, one launch (start us, length us, event | category | flops | bytes accessed | tf_op | source)
XLA Modules:
  0.0 1056.4 jit_solution(10929932766580426875)
XLA Ops:
  27.1 51.8 %all-gather.4.cloned.1.call-done = f32[4,16,9,2048]{3,1,2,0:T(8,128)} async-done(((f32[1,16,9,2048]{3,1,2,0:T(8,128)}), f32[4,16,9,2048]{3,1,2,0:T(8,128)}) %all-gather.4.cloned.1.call-update) | async-done | bytes 4718608 | tf_op jit(solution)/shard_map/all_gather | solution.py:54
  91.5 50.0 %all-to-all-done.1 = f32[8,4,9,2048]{3,1,2,0:T(4,128)S(1)} async-done(((f32[8,4,9,2048]{3,1,2,0:T(4,128)}), f32[8,4,9,2048]{3,1,2,0:T(4,128)S(1)}, u32[]{:S(2)}, u32[]{:S(2)}) %all-to-all-start.1) | async-done | bytes 2359328 | tf_op jit(solution)/shard_map/all_to_all | solution.py:178
  157.9 312.6 %while.24 = (s32[]{:T(128)}, u32[8192]{0:T(1024)S(1)}, u32[8192]{0:T(1024)S(1)}, s32[40]{0:T(128)S(1)}, s32[]{:T(128)}, /*index=5*/s32[]{:T(128)}) while((s32[]{:T(128)}, u32[8192]{0:T(1024)S(1)}, u32[8192]{0:T(1024)S(1)}, s32[40]{0:T(128)S(1)}, s32[]{:T(128)}, /*index=5*/s32[]{:T(128)}) %tuple.233), condition=%wide.region_2.3_spmd.clone, body=%wide.region_1.2_spmd.clone.sunk | while | flops 1392643 | bytes 262864 | solution.py:81
  160.0 25.0 %fusion.150 = u32[8192]{0:T(1024)S(1)} fusion(u32[8192]{0:T(1024)S(1)} %get-tuple-element.525, u32[8192]{0:T(1024)S(1)} %get-tuple-element.524, s32[]{:T(128)} %bitcast.468, s32[]{:T(128)} %bitcast.469, s32[]{:T(128)} %bitcast.470, s32[]{:T(128)} %bitcast.471, s32[]{:T(128)} %bitcast.472, s32[]{:T(128)} %bitcast.473, s32[]{:T(128)} %bitcast.474, ...), kind=kLoop, calls=%fused_computation.8.clone.1 | loop fusion | flops 696320 | bytes 98465 | tf_op jit(solution)/shard_map/jit(searchsorted)/jit(_searchsorted_scan_impl)/vmap(jit(_searchsorted_scan_impl))/while/body/eval_jaxpr/select_n | solution.py:81
  185.0 25.0 %fusion.149 = u32[8192]{0:T(1024)S(1)} fusion(u32[8192]{0:T(1024)S(1)} %get-tuple-element.525, u32[8192]{0:T(1024)S(1)} %get-tuple-element.524, s32[]{:T(128)} %bitcast.468, s32[]{:T(128)} %bitcast.469, s32[]{:T(128)} %bitcast.470, s32[]{:T(128)} %bitcast.471, s32[]{:T(128)} %bitcast.472, s32[]{:T(128)} %bitcast.473, s32[]{:T(128)} %bitcast.474, ...), kind=kLoop, calls=%fused_computation.9.clone.1 | loop fusion | flops 696320 | bytes 98465 | tf_op jit(solution)/shard_map/jit(searchsorted)/jit(_searchsorted_scan_impl)/vmap(jit(_searchsorted_scan_impl))/while/body/eval_jaxpr/select_n | solution.py:81
  212.1 25.0 %fusion.150 = u32[8192]{0:T(1024)S(1)} fusion(u32[8192]{0:T(1024)S(1)} %get-tuple-element.525, u32[8192]{0:T(1024)S(1)} %get-tuple-element.524, s32[]{:T(128)} %bitcast.468, s32[]{:T(128)} %bitcast.469, s32[]{:T(128)} %bitcast.470, s32[]{:T(128)} %bitcast.471, s32[]{:T(128)} %bitcast.472, s32[]{:T(128)} %bitcast.473, s32[]{:T(128)} %bitcast.474, ...), kind=kLoop, calls=%fused_computation.8.clone.1 | loop fusion | flops 696320 | bytes 98465 | tf_op jit(solution)/shard_map/jit(searchsorted)/jit(_searchsorted_scan_impl)/vmap(jit(_searchsorted_scan_impl))/while/body/eval_jaxpr/select_n | solution.py:81
  237.1 25.0 %fusion.149 = u32[8192]{0:T(1024)S(1)} fusion(u32[8192]{0:T(1024)S(1)} %get-tuple-element.525, u32[8192]{0:T(1024)S(1)} %get-tuple-element.524, s32[]{:T(128)} %bitcast.468, s32[]{:T(128)} %bitcast.469, s32[]{:T(128)} %bitcast.470, s32[]{:T(128)} %bitcast.471, s32[]{:T(128)} %bitcast.472, s32[]{:T(128)} %bitcast.473, s32[]{:T(128)} %bitcast.474, ...), kind=kLoop, calls=%fused_computation.9.clone.1 | loop fusion | flops 696320 | bytes 98465 | tf_op jit(solution)/shard_map/jit(searchsorted)/jit(_searchsorted_scan_impl)/vmap(jit(_searchsorted_scan_impl))/while/body/eval_jaxpr/select_n | solution.py:81
  264.2 25.0 %fusion.150 = u32[8192]{0:T(1024)S(1)} fusion(u32[8192]{0:T(1024)S(1)} %get-tuple-element.525, u32[8192]{0:T(1024)S(1)} %get-tuple-element.524, s32[]{:T(128)} %bitcast.468, s32[]{:T(128)} %bitcast.469, s32[]{:T(128)} %bitcast.470, s32[]{:T(128)} %bitcast.471, s32[]{:T(128)} %bitcast.472, s32[]{:T(128)} %bitcast.473, s32[]{:T(128)} %bitcast.474, ...), kind=kLoop, calls=%fused_computation.8.clone.1 | loop fusion | flops 696320 | bytes 98465 | tf_op jit(solution)/shard_map/jit(searchsorted)/jit(_searchsorted_scan_impl)/vmap(jit(_searchsorted_scan_impl))/while/body/eval_jaxpr/select_n | solution.py:81
  289.2 25.0 %fusion.149 = u32[8192]{0:T(1024)S(1)} fusion(u32[8192]{0:T(1024)S(1)} %get-tuple-element.525, u32[8192]{0:T(1024)S(1)} %get-tuple-element.524, s32[]{:T(128)} %bitcast.468, s32[]{:T(128)} %bitcast.469, s32[]{:T(128)} %bitcast.470, s32[]{:T(128)} %bitcast.471, s32[]{:T(128)} %bitcast.472, s32[]{:T(128)} %bitcast.473, s32[]{:T(128)} %bitcast.474, ...), kind=kLoop, calls=%fused_computation.9.clone.1 | loop fusion | flops 696320 | bytes 98465 | tf_op jit(solution)/shard_map/jit(searchsorted)/jit(_searchsorted_scan_impl)/vmap(jit(_searchsorted_scan_impl))/while/body/eval_jaxpr/select_n | solution.py:81
  316.3 25.0 %fusion.150 = u32[8192]{0:T(1024)S(1)} fusion(u32[8192]{0:T(1024)S(1)} %get-tuple-element.525, u32[8192]{0:T(1024)S(1)} %get-tuple-element.524, s32[]{:T(128)} %bitcast.468, s32[]{:T(128)} %bitcast.469, s32[]{:T(128)} %bitcast.470, s32[]{:T(128)} %bitcast.471, s32[]{:T(128)} %bitcast.472, s32[]{:T(128)} %bitcast.473, s32[]{:T(128)} %bitcast.474, ...), kind=kLoop, calls=%fused_computation.8.clone.1 | loop fusion | flops 696320 | bytes 98465 | tf_op jit(solution)/shard_map/jit(searchsorted)/jit(_searchsorted_scan_impl)/vmap(jit(_searchsorted_scan_impl))/while/body/eval_jaxpr/select_n | solution.py:81
  341.3 25.0 %fusion.149 = u32[8192]{0:T(1024)S(1)} fusion(u32[8192]{0:T(1024)S(1)} %get-tuple-element.525, u32[8192]{0:T(1024)S(1)} %get-tuple-element.524, s32[]{:T(128)} %bitcast.468, s32[]{:T(128)} %bitcast.469, s32[]{:T(128)} %bitcast.470, s32[]{:T(128)} %bitcast.471, s32[]{:T(128)} %bitcast.472, s32[]{:T(128)} %bitcast.473, s32[]{:T(128)} %bitcast.474, ...), kind=kLoop, calls=%fused_computation.9.clone.1 | loop fusion | flops 696320 | bytes 98465 | tf_op jit(solution)/shard_map/jit(searchsorted)/jit(_searchsorted_scan_impl)/vmap(jit(_searchsorted_scan_impl))/while/body/eval_jaxpr/select_n | solution.py:81
  368.4 25.0 %fusion.150 = u32[8192]{0:T(1024)S(1)} fusion(u32[8192]{0:T(1024)S(1)} %get-tuple-element.525, u32[8192]{0:T(1024)S(1)} %get-tuple-element.524, s32[]{:T(128)} %bitcast.468, s32[]{:T(128)} %bitcast.469, s32[]{:T(128)} %bitcast.470, s32[]{:T(128)} %bitcast.471, s32[]{:T(128)} %bitcast.472, s32[]{:T(128)} %bitcast.473, s32[]{:T(128)} %bitcast.474, ...), kind=kLoop, calls=%fused_computation.8.clone.1 | loop fusion | flops 696320 | bytes 98465 | tf_op jit(solution)/shard_map/jit(searchsorted)/jit(_searchsorted_scan_impl)/vmap(jit(_searchsorted_scan_impl))/while/body/eval_jaxpr/select_n | solution.py:81
  393.4 25.0 %fusion.149 = u32[8192]{0:T(1024)S(1)} fusion(u32[8192]{0:T(1024)S(1)} %get-tuple-element.525, u32[8192]{0:T(1024)S(1)} %get-tuple-element.524, s32[]{:T(128)} %bitcast.468, s32[]{:T(128)} %bitcast.469, s32[]{:T(128)} %bitcast.470, s32[]{:T(128)} %bitcast.471, s32[]{:T(128)} %bitcast.472, s32[]{:T(128)} %bitcast.473, s32[]{:T(128)} %bitcast.474, ...), kind=kLoop, calls=%fused_computation.9.clone.1 | loop fusion | flops 696320 | bytes 98465 | tf_op jit(solution)/shard_map/jit(searchsorted)/jit(_searchsorted_scan_impl)/vmap(jit(_searchsorted_scan_impl))/while/body/eval_jaxpr/select_n | solution.py:81
  445.5 25.0 %fusion.149 = u32[8192]{0:T(1024)S(1)} fusion(u32[8192]{0:T(1024)S(1)} %get-tuple-element.525, u32[8192]{0:T(1024)S(1)} %get-tuple-element.524, s32[]{:T(128)} %bitcast.468, s32[]{:T(128)} %bitcast.469, s32[]{:T(128)} %bitcast.470, s32[]{:T(128)} %bitcast.471, s32[]{:T(128)} %bitcast.472, s32[]{:T(128)} %bitcast.473, s32[]{:T(128)} %bitcast.474, ...), kind=kLoop, calls=%fused_computation.9.clone.1 | loop fusion | flops 696320 | bytes 98465 | tf_op jit(solution)/shard_map/jit(searchsorted)/jit(_searchsorted_scan_impl)/vmap(jit(_searchsorted_scan_impl))/while/body/eval_jaxpr/select_n | solution.py:81
  486.1 57.0 %scatter_custom_fusion = f32[40]{0:T(128)S(1)} fusion(s32[8192]{0:T(1024)S(1)} %convert_element_type.34, f32[8192]{0:T(1024)S(1)} %add_subtract_fusion.2, f32[]{:T(128)} %constant.148.clone.1), kind=kCustom, calls=%fused_computation.230 | custom fusion | flops 8192 | bytes 164 | tf_op jit(solution)/shard_map/scatter-add | solution.py:203
  545.1 26.0 %fusion.114 = (f32[8192]{0:T(1024)S(1)}, f32[8192]{0:T(1024)S(1)}, pred[8192]{0:T(1024)(128)(4,1)S(1)}, pred[8192]{0:T(1024)(128)(4,1)S(1)}, pred[8192]{0:T(1024...) fusion(f32[8192]{0:T(1024)S(1)} %bitcast.527, ...), kind=kLoop, calls=%fused_computation.235 | loop fusion | flops 712704 | bytes 458912 | tf_op jit(solution)/shard_map/mul | solution.py:212
  578.9 30.9 %all-gather.6.cloned.1.call-done = f32[4,16,3,2048]{3,1,2,0:T(8,128)} async-done(((f32[1,16,3,2048]{3,1,2,0:T(8,128)}), f32[4,16,3,2048]{3,1,2,0:T(8,128)}) %all-gather.6.cloned.1.call-update) | async-done | bytes 1572880 | tf_op jit(solution)/shard_map/all_gather | solution.py:54
  678.9 57.2 %scatter_custom_fusion.1 = f32[40]{0:T(128)S(1)} fusion(s32[8192]{0:T(1024)} %copy-done.1, f32[8192]{0:T(1024)S(1)} %add_subtract_fusion.1, f32[]{:T(128)} %constant.148.clone.1), kind=kCustom, calls=%fused_computation.228 | custom fusion | flops 8192 | bytes 672 | tf_op jit(solution)/shard_map/scatter-add | solution.py:219
  736.6 41.2 %all-reduce = (f32[]{:T(128)}, f32[]{:T(128)}) all-reduce(f32[]{:T(128)} %get-tuple-element.196, f32[]{:T(128)} %get-tuple-element.195), channel_id=1, replica_groups=mesh['det'=4,'obs'=8] {'det','obs'}, use_global_device_ids=true, to_apply=%region_8.10 | all-reduce | flops 2 | bytes 16 | tf_op jit(solution)/shard_map/psum | solution.py:59
  779.8 39.9 %psum.30 = f32[]{:T(128)} all-reduce(f32[]{:T(128)} %get-tuple-element.209), channel_id=1, replica_groups=mesh['det'=4,'obs'=8] {'det','obs'}, use_global_device_ids=true, to_apply=%region_14.17 | all-reduce | flops 1 | bytes 8 | tf_op jit(solution)/shard_map/psum | solution.py:59
  823.1 26.2 %fusion.113 = (f32[8192]{0:T(1024)S(1)}, f32[8192]{0:T(1024)S(1)}) fusion(f32[8192]{0:T(1024)S(1)} %bitcast.529, pred[8192]{0:T(1024)(128)(4,1)} %get-tuple-element.252, pred[8192]{0:T(1024)(128)(4,1)} %get-tuple-element.251, pred[8192]{0:T(1024)(128)(4,1)} %get-tuple-element.250, pred[8192]{0:T(1024)(128)(4,1)} %get-tuple-element.249, ...), kind=kLoop, calls=%fused_computation.234 | loop fusion | flops 335872 | bytes 426144 | tf_op jit(solution)/shard_map/mul | solution.py:212
  857.0 30.8 %all-gather.8.cloned.1.call-done = f32[4,16,3,2048]{3,1,2,0:T(8,128)} async-done(((f32[1,16,3,2048]{3,1,2,0:T(8,128)}), f32[4,16,3,2048]{3,1,2,0:T(8,128)}) %all-gather.8.cloned.1.call-update) | async-done | bytes 1572880 | tf_op jit(solution)/shard_map/all_gather | solution.py:54
  948.3 57.2 %scatter_custom_fusion.2 = f32[40]{0:T(128)S(1)} fusion(s32[8192]{0:T(1024)} %copy-done.1, f32[8192]{0:T(1024)S(1)} %add_subtract_fusion, f32[]{:T(128)} %constant.148.clone.1), kind=kCustom, calls=%fused_computation.226 | custom fusion | flops 8192 | bytes 672 | tf_op jit(solution)/shard_map/scatter-add | solution.py:219
  1006.0 41.2 %psum.31 = f32[]{:T(128)} all-reduce(f32[]{:T(128)} %multiply_reduce_fusion), channel_id=1, replica_groups=mesh['det'=4,'obs'=8] {'det','obs'}, use_global_device_ids=true, to_apply=%region_18.21 | all-reduce | flops 1 | bytes 8 | tf_op jit(solution)/shard_map/psum | solution.py:225
  (189 shorter events, 253.6 us)
Async XLA Ops:
  7.2 7.0 copy-start.9
  7.2 71.7 %all-gather.4.cloned.1.call-start = ((), (), s32[]{:S(2)}) async-start(), calls=%async_computation.7 | async-start | bytes 5898240 | tf_op jit(solution)/shard_map/all_gather | solution.py:54
  17.3 3.4 copy-start.12
  20.9 455.7 %copy-start.2 = (s32[16]{0:T(128)}, s32[16]{0:T(128)S(1)}, u32[]{:S(2)}) copy-start(s32[16]{0:T(128)S(1)} %fusion.103) | copy-start | bytes 196
  21.6 63.2 %all-to-all-start = ((s32[8,1,4]{2,1,0:T(1,128)}), s32[8,1,4]{2,1,0:T(1,128)S(1)}, u32[]{:S(2)}, u32[]{:S(2)}) async-start(s32[8,1,4]{2,1,0:T(1,128)} %bitcast.10), calls=%async_computation | async-start | bytes 8192 | tf_op jit(solution)/shard_map/all_to_all | solution.py:179
  84.8 5.5 copy-start.10
  84.8 56.7 %all-to-all-start.1 = ((f32[8,4,9,2048]{3,1,2,0:T(4,128)}), f32[8,4,9,2048]{3,1,2,0:T(4,128)S(1)}, u32[]{:S(2)}, u32[]{:S(2)}) async-start(f32[8,4,9,2048]{3,1,2,0:T(4,128)} %fusion.34), calls=%async_computation.1 | async-start | bytes 4718592 | tf_op jit(solution)/shard_map/all_to_all | solution.py:178
  150.1 320.5 %all-to-all-start.2 = ((f32[8,4,3,2048]{3,1,2,0:T(4,128)}), f32[8,4,3,2048]{3,1,2,0:T(4,128)}, u32[]{:S(2)}, u32[]{:S(2)}) async-start(f32[8,4,3,2048]{3,1,2,0:T(4,128)} %fusion.17), calls=%async_computation.2 | async-start | bytes 1572864 | tf_op jit(solution)/shard_map/all_to_all | solution.py:196
  157.7 452.2 %all-gather.6.cloned.1.call-start = ((), (), s32[]{:S(2)}) async-start(), calls=%async_computation.8 | async-start | bytes 1966080 | tf_op jit(solution)/shard_map/all_gather | solution.py:54
  470.5 15.6 %copy-start.1 = (s32[8192]{0:T(1024)}, s32[8192]{0:T(1024)S(1)}, u32[]{:S(2)}) copy-start(s32[8192]{0:T(1024)S(1)} %convert_element_type.34) | copy-start | bytes 98308
  470.6 12.8 %copy-start.5 = (s32[1024]{0:T(1024)}, s32[1024]{0:T(1024)S(1)}, u32[]{:S(2)}) copy-start(s32[1024]{0:T(1024)S(1)} %pad_clamp_fusion) | copy-start | bytes 12292
  470.6 14.5 %copy-start.6 = (pred[32]{0:T(512)(128)(4,1)}, pred[32]{0:T(512)(128)(4,1)S(1)}, u32[]{:S(2)}) copy-start(pred[32]{0:T(512)(128)(4,1)S(1)} %compare_and_fusion.1) | copy-start | bytes 100
  481.0 5.1 copy-start
  578.9 308.9 %all-gather.8.cloned.1.call-start = ((), (), s32[]{:S(2)}) async-start(), calls=%async_computation.9 | async-start | bytes 1966080 | tf_op jit(solution)/shard_map/all_gather | solution.py:54
  666.3 2.9 copy-start.3
  672.1 5.7 copy-start.7
  943.1 0.6 copy-start.4
  945.4 1.9 copy-start.8
  945.9 102.6 %copy-start.11 = (s32[1,1,40]{2,1,0:T(1,128)S(1)}, s32[1,1,40]{2,1,0:T(1,128)}, u32[]{:S(2)}) copy-start(s32[1,1,40]{2,1,0:T(1,128)} %param.16) | copy-start | bytes 484
Sparse Core Ops, SparseCore 0:
  20.8 58.0 all-gather.3
  579.0 30.8 all-gather.5
  857.1 30.6 all-gather.7
